TPU v7x, 256 devices: a whole 4x4x8 slice. The times are simulated.
256 devices in a mesh: row: 32 (over x, y, core), col: 8 (over z).
Axes of the slice: x: 4, y: 4, z: 8, core: 2. Of those that a mesh axis runs over, the one named last changes fastest.
Arguments:
- block_values: bfloat16 [32, 8, 192, 128, 128], P('row', 'col'), may hold values from -0.0625 to 0.0625
- block_rows: int32 [32, 8, 192], P('row', 'col'), may hold values from 0 to 4095, as said below
- block_cols: int32 [32, 8, 192], P('row', 'col'), may hold values from 0 to 4095, as said below
- block_counts: int32 [32, 8], P('row', 'col'), may hold values from 48 to 192, as said below
- precond: float32 [8, 512, 128, 128], P('col', 'row')
- right_side: float32 [8, 512, 32, 128], P('col', 'row'), may hold values from -6 to 6
Outputs:
- solution: float32 [8, 512, 32, 128], P('col', 'row')
Inputs may be any that keep to these rules, and one draw needn't show every extreme that they name: `block_rows`: the block rows of device (r, c) lie in [c * 512, (c + 1) * 512); positions may repeat; for each j, at most 9 of a device's 192 slots have (row mod 512) // 16 == j, and in every index of col some j has exactly 9 such slots on every device. `block_cols`: every block column q of device (r, c) has (q mod 512) // 16 == r; positions may repeat. `block_counts`: slots at or past a device's count are unused; some device uses all 192 slots.
All inputs are finite; a program needn't handle non-finite values.
Results may differ from a plain program's by a relative error of at most 0.00073.
Values may be sent and summed in bfloat16 or wider, within the bound.
A program may use at most 64 MiB of HBM per device.

v0:
```python
import jax
import jax.numpy as jnp
from jax import lax
from jax.sharding import PartitionSpec as P

ITERS = 3


def apply_blocks(matrix, field):
    return jnp.einsum("poi,pki->pko", matrix, field, precision=lax.Precision.HIGHEST)


def block_terms(vectors, values, col_local):
    gathered = vectors[col_local]
    return jnp.einsum("ski,soi->sko", gathered, values, preferred_element_type=jnp.float32)


def per_device(block_values, block_rows, block_cols, block_counts, precond, right_side):
    owned = right_side.shape[1]
    row_devices = lax.axis_size("row")
    group = owned * row_devices
    slot_total = block_values.shape[2]
    values = block_values[0, 0]
    row_local = block_rows[0, 0] % group
    col_global = block_cols[0, 0]
    col_local = col_global // group * owned + col_global % owned
    used = block_counts[0, 0]
    live = jnp.arange(slot_total, dtype=jnp.int32) < used
    inverse = precond[0]
    rhs_own = right_side[0]
    solution = apply_blocks(inverse, rhs_own)
    for step in range(ITERS):
        pieces = lax.all_gather(solution.astype(jnp.bfloat16)[None], "col", axis=1, tiled=True)[0]
        terms = block_terms(pieces, values, col_local)
        terms = jnp.where(live[:, None, None], terms, jnp.zeros_like(terms))
        partial_value = jax.ops.segment_sum(terms, row_local, num_segments=group)
        product = lax.psum_scatter(partial_value, "row", scatter_dimension=0, tiled=True)
        residual = rhs_own - solution - product
        solution = solution + apply_blocks(inverse, residual)
    return solution[None]


def solution(mesh):
    placed = (
        P("row", "col", None, None, None),
        P("row", "col", None),
        P("row", "col", None),
        P("row", "col"),
        P("col", "row", None, None),
        P("col", "row", None, None),
    )
    return jax.shard_map(
        per_device,
        mesh=mesh,
        in_specs=placed,
        out_specs=P("col", "row", None, None),
        check_vma=False,
    )
```

profile of v0, /device:TPU:2, one launch (start us, length us, event | category | flops | bytes accessed | tf_op | source)
XLA Modules:
  0.0 562.6 jit_solution(1981962366836233417)
XLA Ops:
  6.5 0.0 copy-start
  6.5 0.0 all-gather.7.cloned.1.call-start
  6.5 1.2 copy-done
  7.8 3.3 fusion.30
  11.1 0.0 all-gather.7.cloned.1.call-update
  11.1 0.0 reduce-scatter.4.cloned.1.call-start
  11.8 0.7 compare_select_fusion
  12.5 0.7 and_select_fusion.2
  13.2 39.4 %all-gather.7.cloned.1.call-done = bf16[128,32,128]{2,1,0:T(8,128)(2,1)} async-done(((bf16[16,32,128]{2,1,0:T(8,128)(2,1)}), bf16[128,32,128]{2,1,0:T(8,128)(2,1)}) %all-gather.7.cloned.1.call-update) | async-done | bytes 1048592 | tf_op jit(solution)/shard_map/all_gather | solution.py:33
  52.6 2.1 gather_fusion
  54.8 7.9 %fusion.6 = f32[192,32,128]{2,1,0:T(8,128)} fusion(bf16[192,32,128]{2,1,0:T(8,128)(2,1)S(1)} %gather_fusion, bf16[1,1,192,128,128]{4,3,2,1,0:T(8,128)(2,1)} %param.6, pred[192]{0:T(512)(128)(4,1)S(1)} %iota_compare_fusion), kind=kOutput, calls=%fused_computation.12 | convolution fusion | flops 202113024 | bytes 11010240 | tf_op jit(solution)/shard_map/ski,soi->sko/dot_general | solution.py:15
  62.7 4.3 broadcast.156.clone
  67.0 25.8 %scatter_fusion = f32[512,32,128]{2,1,0:T(8,128)} fusion(f32[512,32,128]{2,1,0:T(8,128)} %broadcast.156.clone, s32[192]{0:T(256)S(1)} %bitcast.73, f32[192,32,128]{2,1,0:T(8,128)} %fusion.6), kind=kCustom, calls=%fused_computation.3 | custom fusion | flops 786432 | bytes 9437952 | tf_op jit(solution)/shard_map/scatter-add | solution.py:36
  92.8 0.0 copy-start.1
  92.8 0.0 reduce-scatter.4.cloned.1.call-update
  92.9 0.0 all-gather.9.cloned.1.call-start
  92.9 98.6 %reduce-scatter.4.cloned.1.call-done = f32[16,32,128]{2,1,0:T(8,128)} async-done(((f32[512,32,128]{2,1,0:T(8,128)}), f32[16,32,128]{2,1,0:T(8,128)}) %reduce-scatter.4.cloned.1.call-update) | async-done | bytes 262160 | tf_op jit(solution)/shard_map/reduce_scatter | solution.py:37
  191.5 0.0 copy-done.1
  191.5 3.3 fusion.31
  194.8 0.0 all-gather.9.cloned.1.call-update
  194.8 0.0 reduce-scatter.6.cloned.1.call-start
  194.9 38.2 %all-gather.9.cloned.1.call-done = bf16[128,32,128]{2,1,0:T(8,128)(2,1)} async-done(((bf16[16,32,128]{2,1,0:T(8,128)(2,1)}), bf16[128,32,128]{2,1,0:T(8,128)(2,1)}) %all-gather.9.cloned.1.call-update) | async-done | bytes 1048592 | tf_op jit(solution)/shard_map/all_gather | solution.py:33
  233.1 2.1 gather_fusion.1
  235.2 7.9 %fusion.9 = f32[192,32,128]{2,1,0:T(8,128)} fusion(bf16[192,32,128]{2,1,0:T(8,128)(2,1)S(1)} %gather_fusion.1, bf16[1,1,192,128,128]{4,3,2,1,0:T(8,128)(2,1)} %param.6, pred[192]{0:T(512)(128)(4,1)S(1)} %iota_compare_fusion), kind=kOutput, calls=%fused_computation.13 | convolution fusion | flops 202113024 | bytes 11010240 | tf_op jit(solution)/shard_map/ski,soi->sko/dot_general | solution.py:15
  243.1 4.3 broadcast.156.clone.1
  247.4 25.8 %scatter_fusion.1 = f32[512,32,128]{2,1,0:T(8,128)} fusion(f32[512,32,128]{2,1,0:T(8,128)} %broadcast.156.clone.1, s32[192]{0:T(256)S(1)} %bitcast.74, f32[192,32,128]{2,1,0:T(8,128)} %fusion.9), kind=kCustom, calls=%fused_computation.4 | custom fusion | flops 786432 | bytes 9437952 | tf_op jit(solution)/shard_map/scatter-add | solution.py:36
  273.3 0.0 reduce-scatter.6.cloned.1.call-update
  273.3 0.0 all-gather.11.cloned.1.call-start
  273.4 98.6 %reduce-scatter.6.cloned.1.call-done = f32[16,32,128]{2,1,0:T(8,128)} async-done(((f32[512,32,128]{2,1,0:T(8,128)}), f32[16,32,128]{2,1,0:T(8,128)}) %reduce-scatter.6.cloned.1.call-update) | async-done | bytes 262160 | tf_op jit(solution)/shard_map/reduce_scatter | solution.py:37
  371.9 3.3 fusion.32
  375.3 0.0 all-gather.11.cloned.1.call-update
  375.3 0.2 reduce-scatter.8.cloned.1.call-start
  375.5 38.0 %all-gather.11.cloned.1.call-done = bf16[128,32,128]{2,1,0:T(8,128)(2,1)} async-done(((bf16[16,32,128]{2,1,0:T(8,128)(2,1)}), bf16[128,32,128]{2,1,0:T(8,128)(2,1)}) %all-gather.11.cloned.1.call-update) | async-done | bytes 1048592 | tf_op jit(solution)/shard_map/all_gather | solution.py:33
  413.6 2.1 gather_fusion.2
  415.7 7.9 %fusion.12 = f32[192,32,128]{2,1,0:T(8,128)} fusion(bf16[192,32,128]{2,1,0:T(8,128)(2,1)S(1)} %gather_fusion.2, bf16[1,1,192,128,128]{4,3,2,1,0:T(8,128)(2,1)} %param.6, pred[192]{0:T(512)(128)(4,1)S(1)} %iota_compare_fusion), kind=kOutput, calls=%fused_computation.14 | convolution fusion | flops 202113024 | bytes 11010240 | tf_op jit(solution)/shard_map/ski,soi->sko/dot_general | solution.py:15
  423.6 4.3 broadcast.156
  427.9 25.8 %scatter_fusion.2 = f32[512,32,128]{2,1,0:T(8,128)} fusion(f32[512,32,128]{2,1,0:T(8,128)} %broadcast.156, s32[192]{0:T(256)S(1)} %bitcast.75, f32[192,32,128]{2,1,0:T(8,128)} %fusion.12), kind=kCustom, calls=%fused_computation.5 | custom fusion | flops 786432 | bytes 9437952 | tf_op jit(solution)/shard_map/scatter-add | solution.py:36
  453.7 0.0 reduce-scatter.8.cloned.1.call-update
  453.8 98.6 %reduce-scatter.8.cloned.1.call-done = f32[16,32,128]{2,1,0:T(8,128)} async-done(((f32[512,32,128]{2,1,0:T(8,128)}), f32[16,32,128]{2,1,0:T(8,128)}) %reduce-scatter.8.cloned.1.call-update) | async-done | bytes 262160 | tf_op jit(solution)/shard_map/reduce_scatter | solution.py:37
  552.4 3.4 fusion.15
  (2 shorter events, 0.0 us)
Async XLA Ops:
  6.5 1.2 copy-start
  6.5 46.1 %all-gather.7.cloned.1.call-start = ((), (), s32[]{:S(2)}) async-start(), calls=%async_computation.6 | async-start | bytes 1179648 | tf_op jit(solution)/shard_map/all_gather | solution.py:33
  11.1 180.3 %reduce-scatter.4.cloned.1.call-start = ((), (), s32[]{:S(2)}) async-start(), calls=%async_computation.3 | async-start | bytes 8650752 | tf_op jit(solution)/shard_map/reduce_scatter | solution.py:37
  92.8 98.7 %copy-start.1 = (f32[1,16,32,128]{3,2,1,0:T(8,128)S(1)}, f32[1,16,32,128]{3,2,1,0:T(8,128)}, u32[]{:S(2)}) copy-start(f32[1,16,32,128]{3,2,1,0:T(8,128)} %param.11) | copy-start | bytes 786436
  92.9 140.3 %all-gather.9.cloned.1.call-start = ((), (), s32[]{:S(2)}) async-start(), calls=%async_computation.7 | async-start | bytes 1179648 | tf_op jit(solution)/shard_map/all_gather | solution.py:33
  194.8 177.1 %reduce-scatter.6.cloned.1.call-start = ((), (), s32[]{:S(2)}) async-start(), calls=%async_computation.4 | async-start | bytes 8650752 | tf_op jit(solution)/shard_map/reduce_scatter | solution.py:37
  273.3 140.3 %all-gather.11.cloned.1.call-start = ((), (), s32[]{:S(2)}) async-start(), calls=%async_computation.8 | async-start | bytes 1179648 | tf_op jit(solution)/shard_map/all_gather | solution.py:33
  375.3 177.1 %reduce-scatter.8.cloned.1.call-start = ((), (), s32[]{:S(2)}) async-start(), calls=%async_computation.5 | async-start | bytes 8650752 | tf_op jit(solution)/shard_map/reduce_scatter | solution.py:37
Sparse Core Ops, SparseCore 0:
  11.2 41.3 all-gather.6
  93.0 98.4 reduce-scatter.3
  195.0 38.0 all-gather.8
  273.4 98.4 reduce-scatter.5
  375.4 38.0 all-gather.10
  453.9 98.4 reduce-scatter.7
where the time goes:
time: 564 us; the launch traced here: 563 us
  waiting for transfers between devices  412 us (73%)
  other arithmetic  78.9 us (14%)
  matrix products  37.1 us (7%)
  local copies, waits for them, and re-layouts  20.5 us (4%)
  between operations  14.2 us (3%)
    reduce_scatter x3, waiting for transfers between devices, per_device(): lax.psum_scatter(partial_value, 'row', scatter_dimension=0, tiled=True)  296 us
    all_gather x3, waiting for transfers between devices, per_device(): lax.all_gather(solution.astype(jnp.bfloat16)[None], 'col', axis=1, tiled=...  116 us
    scatter-add x3, other arithmetic, per_device(): partial_value = jax.ops.segment_sum(terms, row_local, num_segments=group)  77.5 us
    dot_general x3, matrix products, block_terms(): jnp.einsum('ski,soi->sko', gathered, values, preferred_element_type=jnp.f...  23.7 us
    dot_general x4, matrix products, apply_blocks(): jnp.einsum('poi,pki->pko', matrix, field, precision=lax.Precision.HIGHEST)  13.4 us
    another operation x3, local copies, waits for them, and re-layouts  12.9 us
  transfers between devices with their start and end apart: 6, of which 6 were waited for; matrix products, arithmetic and copies ran while one was open for 0% of the time, Pallas kernels for 0%

commit v1 on v0

--- a/solution.py
+++ b/solution.py
@@ -4,6 +4,11 @@
 from jax.sharding import PartitionSpec as P
 
 ITERS = 3
+
+
+def gather_from_all(array, axis, dim):
+    copies = jnp.concatenate([array] * lax.axis_size(axis), axis=dim)
+    return lax.all_to_all(copies, axis, dim, dim, tiled=True)
 
 
 def apply_blocks(matrix, field):
@@ -30,7 +35,7 @@
     rhs_own = right_side[0]
     solution = apply_blocks(inverse, rhs_own)
     for step in range(ITERS):
-        pieces = lax.all_gather(solution.astype(jnp.bfloat16)[None], "col", axis=1, tiled=True)[0]
+        pieces = gather_from_all(solution.astype(jnp.bfloat16)[None], "col", 1)[0]
         terms = block_terms(pieces, values, col_local)
         terms = jnp.where(live[:, None, None], terms, jnp.zeros_like(terms))
         partial_value = jax.ops.segment_sum(terms, row_local, num_segments=group)

time: 564 us -> 545 us (0.966)
  waiting for transfers between devices: 412 us -> 314 us
  blocking collectives: 0 us -> 66.8 us
  starting transfers between devices: 0.39 us -> 8.59 us
    all_gather x3 -> x0, waiting for transfers between devices: 116 us -> none  [per_device(): lax.all_gather(solution.astype(jnp.bfloat16)[None], 'col', axis=1, tiled=...]
    all_to_all x0 -> x2, blocking collectives: none -> 66.8 us  [gather_from_all(): return lax.all_to_all(copies, axis, dim, dim, tiled=True)]
    all_to_all x0 -> x1, waiting for transfers between devices: none -> 28 us  [gather_from_all(): return lax.all_to_all(copies, axis, dim, dim, tiled=True)]
    reduce_scatter x3, waiting for transfers between devices: 296 us -> 286 us  [per_device(): lax.psum_scatter(partial_value, 'row', scatter_dimension=0, tiled=True)]
    all_to_all x0 -> x1, starting transfers between devices: none -> 8.47 us  [gather_from_all(): return lax.all_to_all(copies, axis, dim, dim, tiled=True)]
  transfers between devices with their start and end apart: 6 -> 4, of which waited for: 6 -> 4; matrix products, arithmetic and copies ran while one was open for 0% -> 0% of each run, Pallas kernels for 0% -> 0%
where the time goes in v1:
time: 545 us; the launch traced here: 544 us
  waiting for transfers between devices  314 us (58%)
  other arithmetic  77.5 us (14%)
  blocking collectives  66.8 us (12%)
  matrix products  37.4 us (7%)
  local copies, waits for them, and re-layouts  25 us (5%)
  between operations  13.9 us (3%)
  starting transfers between devices  8.59 us (2%)
    reduce_scatter x3, waiting for transfers between devices, per_device(): lax.psum_scatter(partial_value, 'row', scatter_dimension=0, tiled=True)  286 us
    scatter-add x3, other arithmetic, per_device(): partial_value = jax.ops.segment_sum(terms, row_local, num_segments=group)  77.5 us
    all_to_all x2, blocking collectives, gather_from_all(): return lax.all_to_all(copies, axis, dim, dim, tiled=True)  66.8 us
    all_to_all x1, waiting for transfers between devices, gather_from_all(): return lax.all_to_all(copies, axis, dim, dim, tiled=True)  28 us
    dot_general x3, matrix products, block_terms(): jnp.einsum('ski,soi->sko', gathered, values, preferred_element_type=jnp.f...  25.3 us
    another operation x3, local copies, waits for them, and re-layouts  12.9 us
    dot_general x4, matrix products, apply_blocks(): jnp.einsum('poi,pki->pko', matrix, field, precision=lax.Precision.HIGHEST)  12.1 us
  transfers between devices with their start and end apart: 4, of which 4 were waited for; matrix products, arithmetic and copies ran while one was open for 0% of the time, Pallas kernels for 0%

profile of v1, /device:TPU:2, one launch (start us, length us, event | category | flops | bytes accessed | tf_op | source)
XLA Modules:
  0.0 543.6 jit_solution(14811353396795390004)
XLA Ops:
  6.5 0.0 copy-start
  6.5 0.0 copy-start.2
  6.5 0.0 copy-start.3
  6.5 1.2 copy-done
  7.8 3.3 bitcast_dynamic-update-slice_fusion.22
  11.1 0.7 bitcast_dynamic-update-slice_fusion.21
  11.8 0.7 bitcast_dynamic-update-slice_fusion.20
  12.4 0.6 bitcast_dynamic-update-slice_fusion.19
  13.1 0.7 bitcast_dynamic-update-slice_fusion.18
  13.7 0.7 bitcast_dynamic-update-slice_fusion.17
  14.4 0.7 bitcast_dynamic-update-slice_fusion.16
  15.1 0.7 bitcast_dynamic-update-slice_fusion.23
  15.7 8.5 %all-to-all-start = ((bf16[1,128,32,128]{3,2,0,1:T(8,128)(2,1)}), bf16[1,128,32,128]{3,2,0,1:T(8,128)(2,1)S(1)}, u32[]{:S(2)}, u32[]{:S(2)}) async-start(bf16[1,128,32,128]{3,2,0,1:T(8,128)(2,1)} %bitcast.6), calls=%async_computation | async-start | bytes 2097152 | tf_op jit(solution)/shard_map/all_to_all | solution.py:11
  24.2 0.0 reduce-scatter.4.cloned.1.call-start
  24.9 0.0 copy-done.2
  25.0 0.0 copy-done.3
  25.0 28.0 %all-to-all-done = bf16[1,128,32,128]{3,2,0,1:T(8,128)(2,1)S(1)} async-done(((bf16[1,128,32,128]{3,2,0,1:T(8,128)(2,1)}), bf16[1,128,32,128]{3,2,0,1:T(8,128)(2,1)S(1)}, u32[]{:S(2)}, u32[]{:S(2)}) %all-to-all-start) | async-done | bytes 1048608 | tf_op jit(solution)/shard_map/all_to_all | solution.py:11
  52.9 2.0 gather_fusion
  54.9 8.4 %fusion.6 = f32[192,32,128]{2,1,0:T(8,128)} fusion(bf16[192,32,128]{2,1,0:T(8,128)(2,1)} %gather_fusion, bf16[1,1,192,128,128]{4,3,2,1,0:T(8,128)(2,1)} %param.6, pred[192]{0:T(512)(128)(4,1)S(1)} %iota_compare_fusion), kind=kOutput, calls=%fused_computation.12 | convolution fusion | flops 202113024 | bytes 11010240 | tf_op jit(solution)/shard_map/ski,soi->sko/dot_general | solution.py:20
  63.4 4.3 broadcast.156.clone
  67.7 25.8 %scatter_fusion = f32[512,32,128]{2,1,0:T(8,128)} fusion(f32[512,32,128]{2,1,0:T(8,128)} %broadcast.156.clone, s32[192]{0:T(256)S(1)} %bitcast.111, f32[192,32,128]{2,1,0:T(8,128)} %fusion.6), kind=kCustom, calls=%fused_computation.3 | custom fusion | flops 786432 | bytes 9437952 | tf_op jit(solution)/shard_map/scatter-add | solution.py:41
  93.5 0.0 copy-start.1
  93.5 0.0 reduce-scatter.4.cloned.1.call-update
  93.5 0.0 reduce-scatter.6.cloned.1.call-start
  93.6 96.6 %reduce-scatter.4.cloned.1.call-done = f32[16,32,128]{2,1,0:T(8,128)} async-done(((f32[512,32,128]{2,1,0:T(8,128)}), f32[16,32,128]{2,1,0:T(8,128)}) %reduce-scatter.4.cloned.1.call-update) | async-done | bytes 262160 | tf_op jit(solution)/shard_map/reduce_scatter | solution.py:42
  190.1 0.0 copy-done.1
  190.1 2.7 bitcast_dynamic-update-slice_fusion.14
  193.0 33.5 %all_to_all.15 = bf16[1,128,32,128]{3,2,0,1:T(8,128)(2,1)S(1)} all-to-all(bf16[1,128,32,128]{3,2,0,1:T(8,128)(2,1)S(1)} %bitcast.109), channel_id=1, replica_groups=mesh['row'=32,'col'=8] {'col'}, dimensions={1} | all-to-all | bytes 2097152 | tf_op jit(solution)/shard_map/all_to_all | solution.py:11
  226.5 2.0 gather_fusion.1
  228.5 8.4 %fusion.9 = f32[192,32,128]{2,1,0:T(8,128)} fusion(bf16[192,32,128]{2,1,0:T(8,128)(2,1)} %gather_fusion.1, bf16[1,1,192,128,128]{4,3,2,1,0:T(8,128)(2,1)} %param.6, pred[192]{0:T(512)(128)(4,1)S(1)} %iota_compare_fusion), kind=kOutput, calls=%fused_computation.13 | convolution fusion | flops 202113024 | bytes 11010240 | tf_op jit(solution)/shard_map/ski,soi->sko/dot_general | solution.py:20
  236.9 4.3 broadcast.156.clone.1
  241.2 25.8 %scatter_fusion.1 = f32[512,32,128]{2,1,0:T(8,128)} fusion(f32[512,32,128]{2,1,0:T(8,128)} %broadcast.156.clone.1, s32[192]{0:T(256)S(1)} %bitcast.112, f32[192,32,128]{2,1,0:T(8,128)} %fusion.9), kind=kCustom, calls=%fused_computation.4 | custom fusion | flops 786432 | bytes 9437952 | tf_op jit(solution)/shard_map/scatter-add | solution.py:41
  267.0 0.0 reduce-scatter.6.cloned.1.call-update
  267.0 0.0 reduce-scatter.8.cloned.1.call-start
  267.1 94.8 %reduce-scatter.6.cloned.1.call-done = f32[16,32,128]{2,1,0:T(8,128)} async-done(((f32[512,32,128]{2,1,0:T(8,128)}), f32[16,32,128]{2,1,0:T(8,128)}) %reduce-scatter.6.cloned.1.call-update) | async-done | bytes 262160 | tf_op jit(solution)/shard_map/reduce_scatter | solution.py:42
  361.9 2.7 bitcast_dynamic-update-slice_fusion.6
  364.8 33.4 %all_to_all.16 = bf16[1,128,32,128]{3,2,0,1:T(8,128)(2,1)S(1)} all-to-all(bf16[1,128,32,128]{3,2,0,1:T(8,128)(2,1)S(1)} %bitcast.110), channel_id=1, replica_groups=mesh['row'=32,'col'=8] {'col'}, dimensions={1} | all-to-all | bytes 2097152 | tf_op jit(solution)/shard_map/all_to_all | solution.py:11
  398.1 2.0 gather_fusion.2
  400.2 8.4 %fusion.12 = f32[192,32,128]{2,1,0:T(8,128)} fusion(bf16[192,32,128]{2,1,0:T(8,128)(2,1)} %gather_fusion.2, bf16[1,1,192,128,128]{4,3,2,1,0:T(8,128)(2,1)} %param.6, pred[192]{0:T(512)(128)(4,1)S(1)} %iota_compare_fusion), kind=kOutput, calls=%fused_computation.14 | convolution fusion | flops 202113024 | bytes 11010240 | tf_op jit(solution)/shard_map/ski,soi->sko/dot_general | solution.py:20
  408.6 4.3 broadcast.156
  412.9 25.8 %scatter_fusion.2 = f32[512,32,128]{2,1,0:T(8,128)} fusion(f32[512,32,128]{2,1,0:T(8,128)} %broadcast.156, s32[192]{0:T(256)S(1)} %bitcast.113, f32[192,32,128]{2,1,0:T(8,128)} %fusion.12), kind=kCustom, calls=%fused_computation.5 | custom fusion | flops 786432 | bytes 9437952 | tf_op jit(solution)/shard_map/scatter-add | solution.py:41
  438.7 0.0 reduce-scatter.8.cloned.1.call-update
  438.7 95.0 %reduce-scatter.8.cloned.1.call-done = f32[16,32,128]{2,1,0:T(8,128)} async-done(((f32[512,32,128]{2,1,0:T(8,128)}), f32[16,32,128]{2,1,0:T(8,128)}) %reduce-scatter.8.cloned.1.call-update) | async-done | bytes 262160 | tf_op jit(solution)/shard_map/reduce_scatter | solution.py:42
  533.7 3.4 fusion.15
  (18 shorter events, 0.3 us)
Async XLA Ops:
  6.5 1.2 copy-start
  6.5 18.4 %copy-start.2 = (s32[1,1,192]{2,1,0:T(1,128)S(1)}, s32[1,1,192]{2,1,0:T(1,128)}, u32[]{:S(2)}) copy-start(s32[1,1,192]{2,1,0:T(1,128)} %param.8) | copy-start | bytes 2308
  6.5 18.4 %copy-start.3 = (s32[1,1,192]{2,1,0:T(1,128)S(1)}, s32[1,1,192]{2,1,0:T(1,128)}, u32[]{:S(2)}) copy-start(s32[1,1,192]{2,1,0:T(1,128)} %param.7) | copy-start | bytes 2308
  15.7 37.2 %all-to-all-start = ((bf16[1,128,32,128]{3,2,0,1:T(8,128)(2,1)}), bf16[1,128,32,128]{3,2,0,1:T(8,128)(2,1)S(1)}, u32[]{:S(2)}, u32[]{:S(2)}) async-start(bf16[1,128,32,128]{3,2,0,1:T(8,128)(2,1)} %bitcast.6), calls=%async_computation | async-start | bytes 2097152 | tf_op jit(solution)/shard_map/all_to_all | solution.py:11
  24.2 165.9 %reduce-scatter.4.cloned.1.call-start = ((), (), s32[]{:S(2)}) async-start(), calls=%async_computation.6 | async-start | bytes 8650752 | tf_op jit(solution)/shard_map/reduce_scatter | solution.py:42
  93.5 96.6 %copy-start.1 = (f32[1,16,32,128]{3,2,1,0:T(8,128)S(1)}, f32[1,16,32,128]{3,2,1,0:T(8,128)}, u32[]{:S(2)}) copy-start(f32[1,16,32,128]{3,2,1,0:T(8,128)} %param.11) | copy-start | bytes 786436
  93.5 268.4 %reduce-scatter.6.cloned.1.call-start = ((), (), s32[]{:S(2)}) async-start(), calls=%async_computation.7 | async-start | bytes 8650752 | tf_op jit(solution)/shard_map/reduce_scatter | solution.py:42
  267.0 266.6 %reduce-scatter.8.cloned.1.call-start = ((), (), s32[]{:S(2)}) async-start(), calls=%async_computation.8 | async-start | bytes 8650752 | tf_op jit(solution)/shard_map/reduce_scatter | solution.py:42
Sparse Core Ops, SparseCore 0:
  93.6 96.4 reduce-scatter.3
  267.2 94.6 reduce-scatter.5
  438.8 94.7 reduce-scatter.7
